TPU v7x, 32 devices: a whole 2x2x4 slice. The times are simulated.
32 devices in a mesh: group: 2 (over y), slab: 8 (over z, x), coil: 2 (over core).
Axes of the slice: x: 2, y: 2, z: 4, core: 2. Of those that a mesh axis runs over, the one named last changes fastest.
Arguments:
- image: float32 [2, 8, 256, 192], P(None, ('group', 'coil'), 'slab'), parts along dimension 1, may hold values from -6 to 6
- noise: float32 [2, 8, 256, 192], P(None, ('group', 'coil'), 'slab'), parts along dimension 1, may hold values from -6 to 6
- coil_maps: bfloat16 [2, 32, 8, 256, 192], P(None, 'coil', 'group', 'slab'), parts along dimension 2, may hold values from -2 to 2
- adjoint_data: float32 [2, 8, 256, 192], P(None, ('group', 'coil'), 'slab'), parts along dimension 1, may hold values from -6 to 6
- sampled_lines: int32 [512, 192], P('group'), parts along dimension 0, may hold values 0 or 1
- lift_weight: float32 [2, 128], replicated, may hold values from -4 to 4
- lift_bias: float32 [128], replicated, may hold values from -4 to 4
- conv_one: bfloat16 [27, 128, 128], replicated, may hold values from -0.109375 to 0.109375
- bias_one: float32 [128], replicated, may hold values from -4 to 4
- conv_two: bfloat16 [27, 128, 128], replicated, may hold values from -0.109375 to 0.109375
- bias_two: float32 [128], replicated, may hold values from -4 to 4
- head_weight: float32 [128, 2], replicated, may hold values from -0.5 to 0.5
- head_bias: float32 [2], replicated, may hold values from -4 to 4
Outputs:
- next_image: float32 [2, 8, 256, 192], P(None, ('group', 'coil'), 'slab'), parts along dimension 1
- dc_gradient: float32 [2, 8, 256, 192], P(None, ('group', 'coil'), 'slab'), parts along dimension 1
There are 2 independent parts, one for each index of `group`. A program takes and returns all parts, laid end to end along the dimension named above; an argument that names none is the same for every part. Nothing has to cross between parts.
All inputs are finite; a program needn't handle non-finite values.
Results may differ from a plain program's by a relative error of at most 0.0015.
Values may be sent and summed in bfloat16 or wider, within the bound.
A program may use at most 192 MiB of HBM per device.

v0:
```python
import math

import jax
import jax.numpy as jnp
from jax import lax
from jax.sharding import PartitionSpec as P

ZB = 96


noise_level = 0.5
step_size = 0.1
data_weight = 2.0


def padded_2(block, sides, width):
    for axis, dim in sides:
        count = lax.axis_size(axis)
        forward = [(i, i + 1) for i in range(count - 1)]
        backward = [(target, source) for source, target in forward]
        low = lax.ppermute(
            lax.slice_in_dim(block, block.shape[dim] - width, None, axis=dim), axis, forward
        )
        high = lax.ppermute(lax.slice_in_dim(block, 0, width, axis=dim), axis, backward)
        block = jnp.concatenate([low, block, high], axis=dim)
    return block


def shortened(value):

    def short(part):
        return part.astype(jnp.bfloat16) if part.dtype == jnp.float32 else part

    return jax.tree.map(short, value)


def dft_table(length):
    indices = jnp.arange(length, dtype=jnp.int32)
    phases = indices[:, None] * indices[None, :] % length
    angles = phases.astype(jnp.float32) * (2.0 * math.pi / length)
    norm_scale = 1.0 / math.sqrt(length)
    return (jnp.cos(angles) * norm_scale, jnp.sin(angles) * norm_scale)


def lift_image(image_part, lift_weight, lift_bias):
    return (
        jnp.einsum("exyz,ec->xyzc", image_part, lift_weight, precision=lax.Precision.HIGHEST)
        + lift_bias
    )


def convolve(padded, weight):
    row_count = padded.shape[0] - 2
    line_count = padded.shape[1] - 2
    z_count = padded.shape[2]
    channels = padded.shape[3]
    padded_z = jnp.pad(padded, ((0, 0), (0, 0), (1, 1), (0, 0)))
    stacked = weight.reshape(9, 3 * channels, weight.shape[2])
    summed = jnp.zeros((row_count, line_count, z_count, weight.shape[2]), jnp.float32)
    for shift_x in range(3):
        for shift_y in range(3):
            columns = jnp.concatenate(
                [
                    padded_z[
                        shift_x : shift_x + row_count,
                        shift_y : shift_y + line_count,
                        shift_z : shift_z + z_count,
                        :,
                    ]
                    for shift_z in range(3)
                ],
                axis=3,
            )
            summed = summed + jnp.einsum(
                "xyzc,cd->xyzd",
                columns,
                stacked[3 * shift_x + shift_y],
                preferred_element_type=jnp.float32,
            )
    return summed


def local(
    image,
    noise,
    coil_maps,
    adjoint_data,
    sampled_lines,
    lift_weight,
    lift_bias,
    conv_one,
    bias_one,
    conv_two,
    bias_two,
    head_weight,
    head_bias,
):
    local_y = image.shape[2]
    z_count = image.shape[3]
    slab_pos = lax.axis_index("slab")
    slab_count = lax.axis_size("slab")
    lift_sum = lift_image(image, lift_weight, lift_bias)
    first_act = jax.nn.elu(lift_sum).astype(jnp.bfloat16)
    padded_one = padded_2(first_act, (("slab", 1), ("coil", 0)), 1)
    inner = convolve(padded_one, conv_one) + bias_one
    second_act = jax.nn.elu(inner).astype(jnp.bfloat16)
    padded_two = padded_2(second_act, (("slab", 1), ("coil", 0)), 1)
    block_sum = lift_sum + convolve(padded_two, conv_two) + bias_two
    score = (
        jnp.einsum(
            "xyzc,ce->exyz", jax.nn.elu(block_sum), head_weight, precision=lax.Precision.HIGHEST
        )
        + head_bias[:, None, None, None]
    ) / noise_level
    whole = lax.all_gather(image, "coil", axis=1, tiled=True)
    maps = coil_maps.astype(jnp.float32)
    maps_re = maps[0]
    maps_im = maps[1]
    coil_re = maps_re * whole[0][None] - maps_im * whole[1][None]
    coil_im = maps_re * whole[1][None] + maps_im * whole[0][None]
    local_coils = maps.shape[1]
    readout = maps.shape[2]
    z_blocks = z_count // ZB
    cos_z, sin_z = dft_table(z_count)
    cos_z = cos_z.reshape(z_count, z_blocks, ZB)
    sin_z = sin_z.reshape(z_count, z_blocks, ZB)
    highest = lax.Precision.HIGHEST
    freq_re = jnp.einsum("cxyz,zbk->bcxyk", coil_re, cos_z, precision=highest) + jnp.einsum(
        "cxyz,zbk->bcxyk", coil_im, sin_z, precision=highest
    )
    freq_im = jnp.einsum("cxyz,zbk->bcxyk", coil_im, cos_z, precision=highest) - jnp.einsum(
        "cxyz,zbk->bcxyk", coil_re, sin_z, precision=highest
    )
    per_device = z_blocks * local_coils * readout // slab_count
    freq_re = freq_re.reshape(slab_count, per_device, local_y, ZB)
    freq_im = freq_im.reshape(slab_count, per_device, local_y, ZB)
    block_index = slab_pos * per_device // (local_coils * readout)
    line_mask = lax.dynamic_slice_in_dim(sampled_lines.astype(jnp.float32), block_index * ZB, ZB, 1)
    cos_y, sin_y = dft_table(sampled_lines.shape[0])
    piece_re = lax.all_to_all(
        freq_re.astype(jnp.bfloat16), "slab", split_axis=0, concat_axis=2, tiled=True
    ).astype(freq_re.dtype)
    piece_im = lax.all_to_all(
        freq_im.astype(jnp.bfloat16), "slab", split_axis=0, concat_axis=2, tiled=True
    ).astype(freq_im.dtype)
    spec_re = jnp.einsum("qy,aiyk->aiqk", cos_y, piece_re, precision=highest) + jnp.einsum(
        "qy,aiyk->aiqk", sin_y, piece_im, precision=highest
    )
    spec_im = jnp.einsum("qy,aiyk->aiqk", cos_y, piece_im, precision=highest) - jnp.einsum(
        "qy,aiyk->aiqk", sin_y, piece_re, precision=highest
    )
    spec_re = spec_re * line_mask
    spec_im = spec_im * line_mask
    back_re = jnp.einsum("qy,aiqk->aiyk", cos_y, spec_re, precision=highest) - jnp.einsum(
        "qy,aiqk->aiyk", sin_y, spec_im, precision=highest
    )
    back_im = jnp.einsum("qy,aiqk->aiyk", cos_y, spec_im, precision=highest) + jnp.einsum(
        "qy,aiqk->aiyk", sin_y, spec_re, precision=highest
    )
    return_re = lax.all_to_all(
        shortened(back_re), "slab", split_axis=2, concat_axis=0, tiled=True
    ).astype(back_re.dtype)
    return_im = lax.all_to_all(
        shortened(back_im), "slab", split_axis=2, concat_axis=0, tiled=True
    ).astype(back_im.dtype)
    return_re = return_re.reshape(z_blocks, local_coils, readout, local_y, ZB)
    return_im = return_im.reshape(z_blocks, local_coils, readout, local_y, ZB)
    field_re = jnp.einsum("bcxyk,zbk->cxyz", return_re, cos_z, precision=highest) - jnp.einsum(
        "bcxyk,zbk->cxyz", return_im, sin_z, precision=highest
    )
    field_im = jnp.einsum("bcxyk,zbk->cxyz", return_im, cos_z, precision=highest) + jnp.einsum(
        "bcxyk,zbk->cxyz", return_re, sin_z, precision=highest
    )
    adjoint_re = jnp.sum(maps_re * field_re + maps_im * field_im, axis=0)
    adjoint_im = jnp.sum(maps_re * field_im - maps_im * field_re, axis=0)
    partial_adjoint = jnp.stack([adjoint_re, adjoint_im])
    own_adjoint = lax.psum_scatter(partial_adjoint, "coil", scatter_dimension=1, tiled=True)
    dc_gradient = own_adjoint - adjoint_data
    next_image = (
        image + step_size * (score - data_weight * dc_gradient) + math.sqrt(2.0 * step_size) * noise
    )
    return (next_image, dc_gradient)


def solution(mesh):
    return jax.shard_map(
        local,
        mesh=mesh,
        in_specs=(
            P(None, ("group", "coil"), "slab", None),
            P(None, ("group", "coil"), "slab", None),
            P(None, "coil", "group", "slab", None),
            P(None, ("group", "coil"), "slab", None),
            P("group", None),
            P(),
            P(),
            P(),
            P(),
            P(),
            P(),
            P(),
            P(),
        ),
        out_specs=(
            P(None, ("group", "coil"), "slab", None),
            P(None, ("group", "coil"), "slab", None),
        ),
        check_vma=False,
    )
```

profile of v0, /device:TPU:3, one launch (start us, length us, event | category | flops | bytes accessed | tf_op | source)
XLA Modules:
  0.0 452.2 jit_solution(515506763225921030)
XLA Ops:
  18.3 6.0 %all-to-all-start.1 = ((bf16[8,16,32,96]{3,2,1,0:T(8,128)(2,1)}), bf16[8,16,32,96]{3,2,1,0:T(8,128)(2,1)}, u32[]{:S(2)}, u32[]{:S(2)}) async-start(bf16[8,16,32,96]{3,2,1,0:T(8,128)(2,1)} %bitcast.83), calls=%async_computation.1 | async-start | bytes 2097152 | tf_op jit(solution)/shard_map/all_to_all | solution.py:143
  24.4 5.1 %fusion.145 = f32[2,96,16,4,32]{1,4,3,2,0:T(8,128)S(1)} fusion(f32[2,16,4,32,192]{4,3,2,1,0:T(8,128)} %copy-done.2, f32[4,32,192]{2,1,0:T(8,128)S(1)} %get-tuple-element.91, f32[4,32,192]{2,1,0:T(8,128)S(1)} %get-tuple-element.90, s32[2,96]{1,0:T(2,128)S(1)} %multiply_add_fusion.3), kind=kOutput, calls=%fused_computation.165 | convolution fusion | flops 907517952 | bytes 4915968 | tf_op jit(solution)/shard_map/cxyz,zbk->bcxyk/dot_general | solution.py:128
  33.3 13.7 %fusion.128 = (bf16[2,32,192,128]{3,2,1,0:T(8,128)(2,1)S(1)}, f32[2,32,192,128]{3,2,1,0:T(8,128)}) fusion(f32[128]{0:T(128)S(1)} %copy-done.73, f32[2,128]{1,0:T(2,128)S(1)} %copy-done, f32[2,2,32,192]{3,2,1,0:T(8,128)S(1)} %copy-done.50), kind=kOutput, calls=%fused_computation.136 | convolution fusion | flops 45613056 | bytes 9537024 | tf_op jit(solution)/shard_map/exyz,ec->xyzc/dot_general | solution.py:47
  63.0 9.1 %collective-permute-done = bf16[2,1,192,128]{3,2,1,0:T(8,128)(2,1)S(1)} collective-permute-done((bf16[2,1,192,128]{3,2,1,0:T(8,128)(2,1)}, bf16[2,1,192,128]{3,2,1,0:T(8,128)(2,1)S(1)}, u32[]{:S(2)}, u32[]{:S(2)}) %collective-permute-start) | collective-permute-done | bytes 98336 | tf_op jit(solution)/shard_map/ppermute | solution.py:21
  75.8 6.8 %collective-permute-start.3 = (bf16[1,34,192,128]{3,2,1,0:T(8,128)(2,1)}, bf16[1,34,192,128]{3,2,1,0:T(8,128)(2,1)}, u32[]{:S(2)}, u32[]{:S(2)}) collective-permute-start(bf16[1,34,192,128]{3,2,1,0:T(8,128)(2,1)} %get-tuple-element.67), channel_id=1, source_target_pairs={{1,0},{3,2},{5,4},{7,6},{9,8},{11,10},{13,12},{15,14},{17,16},{19,... | collective-permute-start | bytes 5013512 | tf_op jit(solution)/shard_map/ppermute | solution.py:24
  105.6 11.7 %all-to-all-start.3 = ((bf16[1,16,256,96]{3,1,0,2:T(8,128)(2,1)}), bf16[1,16,256,96]{3,1,0,2:T(8,128)(2,1)}, u32[]{:S(2)}, u32[]{:S(2)}) async-start(bf16[1,16,256,96]{3,1,0,2:T(8,128)(2,1)} %copy.82), calls=%async_computation.3 | async-start | bytes 2097152 | tf_op jit(solution)/shard_map/all_to_all | solution.py:163
  128.4 9.5 %fusion.122 = bf16[4,34,194,128]{3,2,1,0:T(8,128)(2,1)} fusion(bf16[1,34,192,128]{3,2,1,0:T(8,128)(2,1)} %collective-permute-done.3, bf16[1,34,192,128]{3,2,1,0:T(8,128)(2,1)} %collective-permute-done.2, bf16[2,1,192,128]{3,2,1,0:T(8,128)(2,1)S(1)} %collective-permute-done.1, bf16[2,32,192,128]{3,2,1,0:T(8,128)(2,1)S(1)} %get-tuple-element.92, ...), kind=kLoop, calls=%fused_computation.130 | loop fusion | flops 60788736 | bytes 13438976 | tf_op jit(solution)/shard_map/concatenate | solution.py:25
  137.9 39.5 %fusion.359 = (bf16[2,32,192,128]{3,2,1,0:T(8,128)(2,1)}, bf16[2,32,192,128]{3,2,1,0:T(8,128)(2,1)}, bf16[2,32,192,128]{3,2,1,0:T(8,128)(2,1)}, bf16[2,32,192,12...) fusion(bf16[4,34,194,128]{3,2,1,0:T(8,128)(2,1)} %fusion.122), kind=kLoop, calls=%fused_computation.382 | loop fusion | bytes 113246208 | tf_op jit(solution)/shard_map/slice | solution.py:64
  180.8 6.6 %fusion.362 = (bf16[2,32,192,128]{3,2,1,0:T(8,128)(2,1)}, bf16[2,32,192,128]{3,2,1,0:T(8,128)(2,1)}, bf16[2,32,192,128]{3,2,1,0:T(8,128)(2,1)}, bf16[2,32,192,12...) fusion(bf16[3,34,192,128]{3,2,1,0:T(8,128)(2,1)S(1)} %get-tuple-element.65, ...), kind=kLoop, calls=%fused_computation.385 | loop fusion | bytes 37748736 | tf_op jit(solution)/shard_map/slice | solution.py:64
  187.4 6.9 %fusion.41 = f32[2,32,192,128]{3,2,1,0:T(8,128)} fusion(bf16[384,128,1,1]{1,0,3,2:T(8,128)(2,1)S(1)} %bitcast.324, bf16[2,32,192,128]{3,2,1,0:T(8,128)(2,1)} %get-tuple-element.37, bf16[2,32,192,128]{3,2,1,0:T(8,128)(2,1)S(1)} %get-tuple-element.92, bf16[2,32,192,128]{3,2,1,0:T(8,128)(2,1)} %get-tuple-element.38), kind=kOutput, calls=%fused_computation.47 | convolution fusion | flops 1236271104 | bytes 15826944 | tf_op jit(solution)/shard_map/xyzc,cd->xyzd/dot_general | solution.py:74
  195.3 4.8 %fusion.27 = f32[2,32,192,128]{3,2,1,0:T(8,128)} fusion(bf16[384,128,1,1]{1,0,3,2:T(8,128)(2,1)S(1)} %bitcast.323, bf16[2,32,192,128]{3,2,1,0:T(8,128)(2,1)S(1)} %copy-done.31, bf16[2,32,192,128]{3,2,1,0:T(8,128)(2,1)S(1)} %copy-done.48, bf16[2,32,192,128]{3,2,1,0:T(8,128)(2,1)S(1)} %copy-done.32), kind=kOutput, calls=%fused_computation.33 | convolution fusion | flops 1236271104 | bytes 15826944 | tf_op jit(solution)/shard_map/xyzc,cd->xyzd/dot_general | solution.py:74
  201.3 4.9 %fusion.21 = f32[2,32,192,128]{3,2,1,0:T(8,128)} fusion(bf16[384,128,1,1]{1,0,3,2:T(8,128)(2,1)S(1)} %bitcast.320, bf16[2,32,192,128]{3,2,1,0:T(8,128)(2,1)S(1)} %copy-done.27, bf16[2,32,192,128]{3,2,1,0:T(8,128)(2,1)S(1)} %copy-done.47, bf16[2,32,192,128]{3,2,1,0:T(8,128)(2,1)S(1)} %copy-done.28), kind=kOutput, calls=%fused_computation.27 | convolution fusion | flops 1236271104 | bytes 15826944 | tf_op jit(solution)/shard_map/xyzc,cd->xyzd/dot_general | solution.py:74
  207.3 4.7 %fusion.33 = f32[2,32,192,128]{3,2,1,0:T(8,128)} fusion(bf16[384,128,1,1]{1,0,3,2:T(8,128)(2,1)S(1)} %bitcast.318, bf16[2,32,192,128]{3,2,1,0:T(8,128)(2,1)S(1)} %copy-done.23, bf16[2,32,192,128]{3,2,1,0:T(8,128)(2,1)S(1)} %copy-done.46, bf16[2,32,192,128]{3,2,1,0:T(8,128)(2,1)S(1)} %copy-done.24), kind=kOutput, calls=%fused_computation.39 | convolution fusion | flops 1236271104 | bytes 15826944 | tf_op jit(solution)/shard_map/xyzc,cd->xyzd/dot_general | solution.py:74
  213.3 4.8 %fusion.49 = f32[2,32,192,128]{3,2,1,0:T(8,128)} fusion(bf16[384,128,1,1]{1,0,3,2:T(8,128)(2,1)S(1)} %bitcast.317, bf16[2,32,192,128]{3,2,1,0:T(8,128)(2,1)S(1)} %copy-done.19, bf16[2,32,192,128]{3,2,1,0:T(8,128)(2,1)S(1)} %copy-done.45, bf16[2,32,192,128]{3,2,1,0:T(8,128)(2,1)S(1)} %copy-done.20), kind=kOutput, calls=%fused_computation.55 | convolution fusion | flops 1236271104 | bytes 15826944 | tf_op jit(solution)/shard_map/xyzc,cd->xyzd/dot_general | solution.py:74
  218.1 4.9 %fusion.18 = f32[2,32,192,128]{3,2,1,0:T(8,128)} fusion(bf16[384,128,1,1]{1,0,3,2:T(8,128)(2,1)S(1)} %bitcast.314, bf16[2,32,192,128]{3,2,1,0:T(8,128)(2,1)S(1)} %get-tuple-element.92, bf16[2,1,192,128]{3,2,1,0:T(8,128)(2,1)S(1)} %collective-permute-done, bf16[2,32,192,128]{3,2,1,0:T(8,128)(2,1)S(1)} %copy-done.15, bf16[2,32,192,128]{3,2,1,0:T(8,128)(2,1)S(1)} %copy-done.16), kind=kOutput, calls=%fused_computation.25 | convolution fusion | flops 1245708288 | bytes 15925248 | tf_op jit(solution)/shard_map/xyzc,cd->xyzd/dot_general | solution.py:74
  224.1 4.8 %fusion.55 = f32[2,32,192,128]{3,2,1,0:T(8,128)} fusion(bf16[384,128,1,1]{1,0,3,2:T(8,128)(2,1)S(1)} %bitcast.313, bf16[2,32,192,128]{3,2,1,0:T(8,128)(2,1)S(1)} %copy-done.13, bf16[2,32,192,128]{3,2,1,0:T(8,128)(2,1)S(1)} %copy-done.44, bf16[2,32,192,128]{3,2,1,0:T(8,128)(2,1)S(1)} %copy-done.14), kind=kOutput, calls=%fused_computation.61 | convolution fusion | flops 1236271104 | bytes 15826944 | tf_op jit(solution)/shard_map/xyzc,cd->xyzd/dot_general | solution.py:74
  229.0 4.8 %fusion.13 = f32[2,32,192,128]{3,2,1,0:T(8,128)} fusion(bf16[384,128,1,1]{1,0,3,2:T(8,128)(2,1)S(1)} %bitcast.310, bf16[2,1,192,128]{3,2,1,0:T(8,128)(2,1)S(1)} %collective-permute-done.1, bf16[2,32,192,128]{3,2,1,0:T(8,128)(2,1)S(1)} %get-tuple-element.92, bf16[2,32,192,128]{3,2,1,0:T(8,128)(2,1)S(1)} %copy-done.11, ...), kind=kOutput, calls=%fused_computation.20 | convolution fusion | flops 1245708288 | bytes 15925248 | tf_op jit(solution)/shard_map/xyzc,cd->xyzd/dot_general | solution.py:74
  233.8 5.5 %all-to-all-start.2 = ((bf16[1,16,256,96]{3,1,0,2:T(8,128)(2,1)}), bf16[1,16,256,96]{3,1,0,2:T(8,128)(2,1)}, u32[]{:S(2)}, u32[]{:S(2)}) async-start(bf16[1,16,256,96]{3,1,0,2:T(8,128)(2,1)} %copy.79), calls=%async_computation.2 | async-start | bytes 2097152 | tf_op jit(solution)/shard_map/all_to_all | solution.py:160
  239.3 20.5 %fusion.130 = bf16[2,32,192,128]{3,2,1,0:T(8,128)(2,1)S(1)} fusion(f32[2,32,192,128]{3,2,1,0:T(8,128)} %fusion.55, f32[2,32,192,128]{3,2,1,0:T(8,128)} %fusion.49, f32[2,32,192,128]{3,2,1,0:T(8,128)} %fusion.13, f32[2,32,192,128]{3,2,1,0:T(8,128)} %fusion.41, f32[2,32,192,128]{3,2,1,0:T(8,128)} %fusion.18, f32[2,32,192,128]{3,2,1,0:T(8,128)} %fusion.33, ...), kind=kOutput, calls=%fused_computation.138 | convolution fusion | flops 1256718336 | bytes 63013376 | tf_op jit(solution)/shard_map/xyzc,cd->xyzd/dot_general | solution.py:74
  274.2 5.8 %collective-permute-start.7 = (bf16[1,34,192,128]{3,2,1,0:T(8,128)(2,1)}, bf16[1,34,192,128]{3,2,1,0:T(8,128)(2,1)}, u32[]{:S(2)}, u32[]{:S(2)}) collective-permute-start(bf16[1,34,192,128]{3,2,1,0:T(8,128)(2,1)} %get-tuple-element.63), channel_id=1, source_target_pairs={{1,0},{3,2},{5,4},{7,6},{9,8},{11,10},{13,12},{15,14},{17,16},{19,... | collective-permute-start | bytes 5013512 | tf_op jit(solution)/shard_map/ppermute | solution.py:24
  296.5 5.6 %maximum_maximum_fusion.1 = (bf16[3,34,192,128]{3,2,1,0:T(8,128)(2,1)S(1)}, bf16[3,34,192,128]{3,2,1,0:T(8,128)(2,1)}) fusion(bf16[2,1,192,128]{3,2,1,0:T(8,128)(2,1)S(1)} %collective-permute-done.5, bf16[2,32,192,128]{3,2,1,0:T(8,128)(2,1)S(1)} %fusion.130, bf16[2,1,192,128]{3,2,1,0:T(8,128)(2,1)S(1)} %collective-permute-done.4, ...), kind=kLoop, calls=%fused_computation.148 | loop fusion | flops 15040512 | bytes 16711680 | tf_op jit(solution)/shard_map/concatenate | solution.py:25
  306.0 9.5 %select_maximum_fusion = bf16[4,34,194,128]{3,2,1,0:T(8,128)(2,1)} fusion(bf16[1,34,192,128]{3,2,1,0:T(8,128)(2,1)} %collective-permute-done.7, bf16[1,34,192,128]{3,2,1,0:T(8,128)(2,1)} %collective-permute-done.6, bf16[2,1,192,128]{3,2,1,0:T(8,128)(2,1)S(1)} %collective-permute-done.5, bf16[2,32,192,128]{3,2,1,0:T(8,128)(2,1)S(1)} %fusion.130, ...), kind=kLoop, calls=%fused_computation.119 | loop fusion | flops 60788736 | bytes 13438976 | tf_op jit(solution)/shard_map/concatenate | solution.py:25
  315.6 39.5 %fusion.358 = (bf16[2,32,192,128]{3,2,1,0:T(8,128)(2,1)}, bf16[2,32,192,128]{3,2,1,0:T(8,128)(2,1)}, bf16[2,32,192,128]{3,2,1,0:T(8,128)(2,1)}, bf16[2,32,192,12...) fusion(bf16[4,34,194,128]{3,2,1,0:T(8,128)(2,1)} %select_maximu, ...), kind=kLoop, calls=%fused_computation.381 | loop fusion | bytes 113246208 | tf_op jit(solution)/shard_map/slice | solution.py:64
  355.1 5.6 %fusion.360 = (bf16[2,32,192,128]{3,2,1,0:T(8,128)(2,1)}, bf16[2,32,192,128]{3,2,1,0:T(8,128)(2,1)S(1)}, bf16[2,32,192,128]{3,2,1,0:T(8,128)(2,1)S(1)}) fusion(bf16[3,34,192,128]{3,2,1,0:T(8,128)(2,1)} %get-tuple-element.61), kind=kLoop, calls=%fused_computation.383 | loop fusion | bytes 18874368 | tf_op jit(solution)/shard_map/slice | solution.py:64
  361.9 4.8 %fusion.87 = f32[2,32,192,128]{3,2,1,0:T(8,128)} fusion(bf16[384,128,1,1]{1,0,3,2:T(8,128)(2,1)S(1)} %bitcast.322, bf16[2,32,192,128]{3,2,1,0:T(8,128)(2,1)S(1)} %copy-done.39, bf16[2,32,192,128]{3,2,1,0:T(8,128)(2,1)S(1)} %fusion.130, bf16[2,32,192,128]{3,2,1,0:T(8,128)(2,1)S(1)} %copy-done.40), kind=kOutput, calls=%fused_computation.93 | convolution fusion | flops 1236271104 | bytes 15826944 | tf_op jit(solution)/shard_map/xyzc,cd->xyzd/dot_general | solution.py:74
  367.9 4.7 %fusion.73 = f32[2,32,192,128]{3,2,1,0:T(8,128)} fusion(bf16[384,128,1,1]{1,0,3,2:T(8,128)(2,1)S(1)} %bitcast.321, bf16[2,32,192,128]{3,2,1,0:T(8,128)(2,1)S(1)} %copy-done.37, bf16[2,32,192,128]{3,2,1,0:T(8,128)(2,1)S(1)} %copy-done.43, bf16[2,32,192,128]{3,2,1,0:T(8,128)(2,1)S(1)} %copy-done.38), kind=kOutput, calls=%fused_computation.79 | convolution fusion | flops 1236271104 | bytes 15826944 | tf_op jit(solution)/shard_map/xyzc,cd->xyzd/dot_general | solution.py:74
  373.9 4.8 %fusion.67 = f32[2,32,192,128]{3,2,1,0:T(8,128)} fusion(bf16[384,128,1,1]{1,0,3,2:T(8,128)(2,1)S(1)} %bitcast.319, bf16[2,32,192,128]{3,2,1,0:T(8,128)(2,1)S(1)} %copy-done.35, bf16[2,32,192,128]{3,2,1,0:T(8,128)(2,1)S(1)} %copy-done.42, bf16[2,32,192,128]{3,2,1,0:T(8,128)(2,1)S(1)} %copy-done.36), kind=kOutput, calls=%fused_computation.73 | convolution fusion | flops 1236271104 | bytes 15826944 | tf_op jit(solution)/shard_map/xyzc,cd->xyzd/dot_general | solution.py:74
  389.2 4.8 %fusion.101 = f32[2,32,192,128]{3,2,1,0:T(8,128)} fusion(bf16[384,128,1,1]{1,0,3,2:T(8,128)(2,1)S(1)} %bitcast.312, bf16[2,32,192,128]{3,2,1,0:T(8,128)(2,1)S(1)} %copy-done.25, bf16[2,32,192,128]{3,2,1,0:T(8,128)(2,1)S(1)} %get-tuple-element.49, bf16[2,32,192,128]{3,2,1,0:T(8,128)(2,1)S(1)} %copy-done.26), kind=kOutput, calls=%fused_computation.107 | convolution fusion | flops 1236271104 | bytes 15826944 | tf_op jit(solution)/shard_map/xyzc,cd->xyzd/dot_general | solution.py:74
  394.0 5.0 %fusion.8 = f32[2,32,192,128]{3,2,1,0:T(8,128)} fusion(bf16[384,128,1,1]{1,0,3,2:T(8,128)(2,1)S(1)} %bitcast.311, bf16[2,32,192,128]{3,2,1,0:T(8,128)(2,1)S(1)} %fusion.130, bf16[2,1,192,128]{3,2,1,0:T(8,128)(2,1)S(1)} %collective-permute-done.4, bf16[2,32,192,128]{3,2,1,0:T(8,128)(2,1)S(1)} %copy-done.21, bf16[2,32,192,128]{3,2,1,0:T(8,128)(2,1)S(1)} %copy-done.22), kind=kOutput, calls=%fused_computation.15 | convolution fusion | flops 1245708288 | bytes 15925248 | tf_op jit(solution)/shard_map/xyzc,cd->xyzd/dot_general | solution.py:74
  399.1 4.8 %fusion.3 = f32[2,32,192,128]{3,2,1,0:T(8,128)} fusion(bf16[384,128,1,1]{1,0,3,2:T(8,128)(2,1)S(1)} %bitcast.309, bf16[2,1,192,128]{3,2,1,0:T(8,128)(2,1)S(1)} %collective-permute-done.5, bf16[2,32,192,128]{3,2,1,0:T(8,128)(2,1)S(1)} %fusion.130, bf16[2,32,192,128]{3,2,1,0:T(8,128)(2,1)S(1)} %copy-done.17, bf16[2,32,192,128]{3,2,1,0:T(8,128)(2,1)S(1)} %copy-done.18), kind=kOutput, calls=%fused_computation.10 | convolution fusion | flops 1245708288 | bytes 15925248 | tf_op jit(solution)/shard_map/xyzc,cd->xyzd/dot_general | solution.py:74
  404.0 24.8 %convert_reduce_fusion = (u32[2,192,128]{2,1,0:T(8,128)S(1)}, f32[2,32,192,128]{3,2,1,0:T(8,128)}) fusion(f32[128]{0:T(128)S(1)} %copy-done.72, bf16[384,128,1,1]{1,0,3,2:T(8,128)(2,1)S(1)} %bitcast.308, bf16[2,32,192,128]{3,2,1,0:T(8,128)(2,1)} %get-tuple-element.29, bf16[2,32,192,128]{3,2,1,0:T(8,128)(2,1)} %get-tuple-element.48, ...), kind=kOutput, calls=%fused_computation.143 | convolution fusion | flops 1259814912 | bytes 72647680 | tf_op jit(solution)/shard_map/xyzc,cd->xyzd/dot_general | solution.py:74
  428.8 14.6 %fusion.134 = f32[2,32,192,2]{2,3,1,0:T(2,128)S(1)} fusion(f32[2,32,192,128]{3,2,1,0:T(8,128)} %get-tuple-element.95, u32[2,192,128]{2,1,0:T(8,128)S(1)} %get-tuple-element.94, f32[128,2]{0,1:T(2,128)S(1)} %copy-done.76), kind=kOutput, calls=%fused_computation.145 | convolution fusion | flops 45613056 | bytes 6587392 | tf_op jit(solution)/shard_map/xyzc,ce->exyz/dot_general | solution.py:110
  (218 shorter events, 128.2 us)
Async XLA Ops:
  7.2 26.1 %copy-start = (f32[2,128]{1,0:T(2,128)S(1)}, f32[2,128]{1,0:T(2,128)}, u32[]{:S(2)}) copy-start(f32[2,128]{1,0:T(2,128)} %param.18) | copy-start | bytes 3076
  7.2 22.3 %copy-start.69 = (s32[2,96]{1,0:T(2,128)}, s32[2,96]{1,0:T(2,128)S(1)}, u32[]{:S(2)}) copy-start(s32[2,96]{1,0:T(2,128)S(1)} %multiply_add_fusion.3) | copy-start | bytes 2308
  9.4 9.0 %copy-start.2 = (f32[2,16,4,32,192]{4,3,2,1,0:T(8,128)}, f32[2,16,4,32,192]{4,3,2,1,0:T(8,128)S(1)}, u32[]{:S(2)}) copy-start(f32[2,16,4,32,192]{4,3,2,1,0:T(8,128)S(1)} %convert_element_type.140) | copy-start | bytes 9437188
  18.3 31.1 %all-to-all-start.1 = ((bf16[8,16,32,96]{3,2,1,0:T(8,128)(2,1)}), bf16[8,16,32,96]{3,2,1,0:T(8,128)(2,1)}, u32[]{:S(2)}, u32[]{:S(2)}) async-start(bf16[8,16,32,96]{3,2,1,0:T(8,128)(2,1)} %bitcast.83), calls=%async_computation.1 | async-start | bytes 2097152 | tf_op jit(solution)/shard_map/all_to_all | solution.py:143
  24.4 8.9 %copy-start.73 = (f32[128]{0:T(128)S(1)}, f32[128]{0:T(128)}, u32[]{:S(2)}) copy-start(f32[128]{0:T(128)} %param.19) | copy-start | bytes 1540
  49.4 38.7 %all-to-all-start = ((bf16[8,16,32,96]{3,2,1,0:T(8,128)(2,1)}), bf16[8,16,32,96]{3,2,1,0:T(8,128)(2,1)}, u32[]{:S(2)}, u32[]{:S(2)}) async-start(bf16[8,16,32,96]{3,2,1,0:T(8,128)(2,1)} %bitcast.304), calls=%async_computation | async-start | bytes 2097152 | tf_op jit(solution)/shard_map/all_to_all | solution.py:140
  54.7 17.5 %collective-permute-start = (bf16[2,1,192,128]{3,2,1,0:T(8,128)(2,1)}, bf16[2,1,192,128]{3,2,1,0:T(8,128)(2,1)S(1)}, u32[]{:S(2)}, u32[]{:S(2)}) collective-permute-start(bf16[2,1,192,128]{3,2,1,0:T(8,128)(2,1)} %get-tuple-element.70), channel_id=1, source_target_pairs={{0,2},{2,4},{4,6},{6,8},{8,10},{10,12},{12,14},{1,3},{3,5},{5,7},{... | collective-permute-start | bytes 294920 | tf_op jit(solution)/shard_map/ppermute | solution.py:21
  57.8 14.4 %collective-permute-start.1 = (bf16[2,1,192,128]{3,2,1,0:T(8,128)(2,1)}, bf16[2,1,192,128]{3,2,1,0:T(8,128)(2,1)S(1)}, u32[]{:S(2)}, u32[]{:S(2)}) collective-permute-start(bf16[2,1,192,128]{3,2,1,0:T(8,128)(2,1)} %get-tuple-element.71), channel_id=1, source_target_pairs={{2,0},{4,2},{6,4},{8,6},{10,8},{12,10},{14,12},{3,1},{5,3},{7,5},{... | collective-permute-start | bytes 294920 | tf_op jit(solution)/shard_map/ppermute | solution.py:24
  74.5 53.9 %collective-permute-start.2 = (bf16[1,34,192,128]{3,2,1,0:T(8,128)(2,1)}, bf16[1,34,192,128]{3,2,1,0:T(8,128)(2,1)}, u32[]{:S(2)}, u32[]{:S(2)}) collective-permute-start(bf16[1,34,192,128]{3,2,1,0:T(8,128)(2,1)} %get-tuple-element.66), channel_id=1, source_target_pairs={{0,1},{2,3},{4,5},{6,7},{8,9},{10,11},{12,13},{14,15},{16,17},{18,... | collective-permute-start | bytes 5013512 | tf_op jit(solution)/shard_map/ppermute | solution.py:21
  75.8 52.6 %collective-permute-start.3 = (bf16[1,34,192,128]{3,2,1,0:T(8,128)(2,1)}, bf16[1,34,192,128]{3,2,1,0:T(8,128)(2,1)}, u32[]{:S(2)}, u32[]{:S(2)}) collective-permute-start(bf16[1,34,192,128]{3,2,1,0:T(8,128)(2,1)} %get-tuple-element.67), channel_id=1, source_target_pairs={{1,0},{3,2},{5,4},{7,6},{9,8},{11,10},{13,12},{15,14},{17,16},{19,... | collective-permute-start | bytes 5013512 | tf_op jit(solution)/shard_map/ppermute | solution.py:24
  88.1 7.0 %copy-start.9 = (bf16[1,16,8,32,96]{4,3,2,1,0:T(8,128)(2,1)S(1)}, bf16[1,16,8,32,96]{4,3,2,1,0:T(8,128)(2,1)}, u32[]{:S(2)}) copy-start(bf16[1,16,8,32,96]{4,3,2,1,0:T(8,128)(2,1)} %copy-done.8) | copy-start | bytes 2359300
  105.6 128.2 %all-to-all-start.3 = ((bf16[1,16,256,96]{3,1,0,2:T(8,128)(2,1)}), bf16[1,16,256,96]{3,1,0,2:T(8,128)(2,1)}, u32[]{:S(2)}, u32[]{:S(2)}) async-start(bf16[1,16,256,96]{3,1,0,2:T(8,128)(2,1)} %copy.82), calls=%async_computation.3 | async-start | bytes 2097152 | tf_op jit(solution)/shard_map/all_to_all | solution.py:163
  187.4 6.9 %copy-start.31 = (bf16[2,32,192,128]{3,2,1,0:T(8,128)(2,1)S(1)}, bf16[2,32,192,128]{3,2,1,0:T(8,128)(2,1)}, u32[]{:S(2)}) copy-start(bf16[2,32,192,128]{3,2,1,0:T(8,128)(2,1)} %get-tuple-element.43) | copy-start | bytes 9437188
  187.4 6.9 %copy-start.32 = (bf16[2,32,192,128]{3,2,1,0:T(8,128)(2,1)S(1)}, bf16[2,32,192,128]{3,2,1,0:T(8,128)(2,1)}, u32[]{:S(2)}) copy-start(bf16[2,32,192,128]{3,2,1,0:T(8,128)(2,1)} %get-tuple-element.44) | copy-start | bytes 9437188
  187.4 7.9 %copy-start.48 = (bf16[2,32,192,128]{3,2,1,0:T(8,128)(2,1)S(1)}, bf16[2,32,192,128]{3,2,1,0:T(8,128)(2,1)}, u32[]{:S(2)}) copy-start(bf16[2,32,192,128]{3,2,1,0:T(8,128)(2,1)} %get-tuple-element.98) | copy-start | bytes 9437188
  187.4 7.9 %copy-start.67 = (bf16[3,128,128]{2,1,0:T(8,128)(2,1)S(1)}, bf16[3,128,128]{2,1,0:T(8,128)(2,1)}, u32[]{:S(2)}) copy-start(bf16[3,128,128]{2,1,0:T(8,128)(2,1)} %get-tuple-element.87) | copy-start | bytes 294916
  229.0 10.3 %copy-start.52 = (bf16[3,128,128]{2,1,0:T(8,128)(2,1)S(1)}, bf16[3,128,128]{2,1,0:T(8,128)(2,1)}, u32[]{:S(2)}) copy-start(bf16[3,128,128]{2,1,0:T(8,128)(2,1)} %get-tuple-element.81) | copy-start | bytes 294916
  229.0 10.3 %copy-start.71 = (f32[128]{0:T(128)S(1)}, f32[128]{0:T(128)}, u32[]{:S(2)}) copy-start(f32[128]{0:T(128)} %param.21) | copy-start | bytes 1540
  233.8 51.9 %all-to-all-start.2 = ((bf16[1,16,256,96]{3,1,0,2:T(8,128)(2,1)}), bf16[1,16,256,96]{3,1,0,2:T(8,128)(2,1)}, u32[]{:S(2)}, u32[]{:S(2)}) async-start(bf16[1,16,256,96]{3,1,0,2:T(8,128)(2,1)} %copy.79), calls=%async_computation.2 | async-start | bytes 2097152 | tf_op jit(solution)/shard_map/all_to_all | solution.py:160
  239.3 204.1 %reduce-scatter.2.cloned.1.call-start = ((), (), s32[]{:S(2)}) async-start(), calls=%async_computation.5 | async-start | bytes 393216 | tf_op jit(solution)/shard_map/reduce_scatter | solution.py:177
  239.3 25.8 %copy-start.49 = (bf16[27,128,128]{2,1,0:T(8,128)(2,1)S(1)}, bf16[27,128,128]{2,1,0:T(8,128)(2,1)}, u32[]{:S(2)}) copy-start(bf16[27,128,128]{2,1,0:T(8,128)(2,1)} %param.22) | copy-start | bytes 2654212
  259.8 6.2 %collective-permute-start.4 = (bf16[2,1,192,128]{3,2,1,0:T(8,128)(2,1)S(1)}, bf16[2,1,192,128]{3,2,1,0:T(8,128)(2,1)S(1)}, u32[]{:S(2)}, u32[]{:S(2)}) collective-permute-start(bf16[2,1,192,128]{3,2,1,0:T(8,128)(2,1)S(1)} %get-tuple-element.68), channel_id=1, source_target_pairs={{0,2},{2,4},{4,6},{6,8},{8,10},{10,12},{12,14},{1,3},{3,5},{5,7},{... | collective-permute-start | bytes 294920 | tf_op jit(solution)/shard_map/ppermute | solution.py:21
  262.9 7.6 %collective-permute-start.5 = (bf16[2,1,192,128]{3,2,1,0:T(8,128)(2,1)S(1)}, bf16[2,1,192,128]{3,2,1,0:T(8,128)(2,1)S(1)}, u32[]{:S(2)}, u32[]{:S(2)}) collective-permute-start(bf16[2,1,192,128]{3,2,1,0:T(8,128)(2,1)S(1)} %get-tuple-element.69), channel_id=1, source_target_pairs={{2,0},{4,2},{6,4},{8,6},{10,8},{12,10},{14,12},{3,1},{5,3},{7,5},{... | collective-permute-start | bytes 294920 | tf_op jit(solution)/shard_map/ppermute | solution.py:24
  270.9 11.7 %copy-start.70 = (s32[2,96]{1,0:T(2,128)S(1)}, s32[2,96]{1,0:T(2,128)}, u32[]{:S(2)}) copy-start(s32[2,96]{1,0:T(2,128)} %copy-done.69) | copy-start | bytes 2308
  272.9 23.6 %collective-permute-start.6 = (bf16[1,34,192,128]{3,2,1,0:T(8,128)(2,1)}, bf16[1,34,192,128]{3,2,1,0:T(8,128)(2,1)}, u32[]{:S(2)}, u32[]{:S(2)}) collective-permute-start(bf16[1,34,192,128]{3,2,1,0:T(8,128)(2,1)} %get-tuple-element.62), channel_id=1, source_target_pairs={{0,1},{2,3},{4,5},{6,7},{8,9},{10,11},{12,13},{14,15},{16,17},{18,... | collective-permute-start | bytes 5013512 | tf_op jit(solution)/shard_map/ppermute | solution.py:21
  274.2 22.3 %collective-permute-start.7 = (bf16[1,34,192,128]{3,2,1,0:T(8,128)(2,1)}, bf16[1,34,192,128]{3,2,1,0:T(8,128)(2,1)}, u32[]{:S(2)}, u32[]{:S(2)}) collective-permute-start(bf16[1,34,192,128]{3,2,1,0:T(8,128)(2,1)} %get-tuple-element.63), channel_id=1, source_target_pairs={{1,0},{3,2},{5,4},{7,6},{9,8},{11,10},{13,12},{15,14},{17,16},{19,... | collective-permute-start | bytes 5013512 | tf_op jit(solution)/shard_map/ppermute | solution.py:24
  403.9 24.8 %copy-start.76 = (f32[128,2]{0,1:T(2,128)S(1)}, f32[128,2]{0,1:T(2,128)}, u32[]{:S(2)}) copy-start(f32[128,2]{0,1:T(2,128)} %param.24) | copy-start | bytes 3076
  428.7 16.4 %copy-start.1 = (f32[2,128]{1,0:T(2,128)S(1)}, f32[2,128]{1,0:T(2,128)}, u32[]{:S(2)}) copy-start(f32[2,128]{1,0:T(2,128)} %param.18) | copy-start | bytes 3076
  428.7 14.7 %copy-start.51 = (f32[2,2,32,192]{3,2,1,0:T(8,128)S(1)}, f32[2,2,32,192]{3,2,1,0:T(8,128)}, u32[]{:S(2)}) copy-start(f32[2,2,32,192]{3,2,1,0:T(8,128)} %param.13) | copy-start | bytes 294916
  428.7 14.7 %copy-start.54 = (f32[2,2,32,192]{3,2,1,0:T(8,128)S(1)}, f32[2,2,32,192]{3,2,1,0:T(8,128)}, u32[]{:S(2)}) copy-start(f32[2,2,32,192]{3,2,1,0:T(8,128)} %param.14) | copy-start | bytes 294916
  428.7 14.7 %copy-start.55 = (f32[2,2,32,192]{3,2,1,0:T(8,128)S(1)}, f32[2,2,32,192]{3,2,1,0:T(8,128)}, u32[]{:S(2)}) copy-start(f32[2,2,32,192]{3,2,1,0:T(8,128)} %param.16) | copy-start | bytes 294916
  428.8 14.7 %copy-start.75 = (f32[2]{0:T(128)S(1)}, f32[2]{0:T(128)}, u32[]{:S(2)}) copy-start(f32[2]{0:T(128)} %param.25) | copy-start | bytes 28
  (58 other events, 295.8 us)
Sparse Core Ops, SparseCore 0:
  296.6 7.9 reduce-scatter.1
where the time goes:
time: 458 us; the launch traced here: 452 us
  matrix products  203 us (44%)
  local copies, waits for them, and re-layouts  126 us (28%)
  starting transfers between devices  53.4 us (12%)
  other arithmetic  36 us (8%)
  waiting for transfers between devices  16 us (3%)
  between operations  15.1 us (3%)
    dot_general x18, matrix products, convolve(): jnp.einsum('xyzc,cd->xyzd', columns, stacked[3 * shift_x + shift_y], pref...  124 us
    slice x5, local copies, waits for them, and re-layouts, convolve(): padded_z[shift_x:shift_x + row_count, shift_y:shift_y + line_count, shift...  95.1 us
    concatenate x6, other arithmetic, padded_2(): block = jnp.concatenate([low, block, high], axis=dim)  29 us
    ppermute x4, starting transfers between devices, padded_2(): lax.ppermute(lax.slice_in_dim(block, 0, width, axis=dim), axis, backward)  17 us
    dot_general x1, matrix products, local(): jnp.einsum('xyzc,ce->exyz', jax.nn.elu(block_sum), head_weight, precision...  14.6 us
    dot_general x1, matrix products, lift_image(): jnp.einsum('exyz,ec->xyzc', image_part, lift_weight, precision=lax.Precis...  13.7 us
    unnamed x154, local copies, waits for them, and re-layouts  12.7 us
    all_to_all x1, starting transfers between devices, local(): lax.all_to_all(shortened(back_im), 'slab', split_axis=2, concat_axis=0, t...  11.7 us
  transfers between devices with their start and end apart: 13, of which 3 were waited for; matrix products, arithmetic and copies ran while one was open for 76% of the time, Pallas kernels for 0%

commit v1 on v0

v1 whole, which is shorter than its diff:
```python
import functools
import math

import jax
import jax.numpy as jnp
import numpy as np
from jax import lax
from jax.experimental import pallas as pl
from jax.experimental.pallas import tpu as pltpu
from jax.sharding import PartitionSpec as P

noise_level = 0.5
step_size = 0.1
data_weight = 2.0
LANES = 128
VMEM_LIMIT = 58 * 1024 * 1024


def elu(value):
    return jnp.where(value > 0, value, jnp.exp(jnp.minimum(value, 0.0)) - 1.0)


def halves(value):
    high = value.astype(jnp.bfloat16)
    low = (value - high.astype(jnp.float32)).astype(jnp.bfloat16)
    return high, low


def split_halves(value):
    high = lax.reduce_precision(value, 8, 7)
    return high.astype(jnp.bfloat16), (value - high).astype(jnp.bfloat16)


def swap_coil(value):
    return lax.ppermute(value, "coil", [(0, 1), (1, 0)])


def store_shifted(scratch, line, value):
    depth, width = value.shape
    position = lax.broadcasted_iota(jnp.int32, value.shape, 0)
    before = jnp.where(position == 0, 0.0, pltpu.roll(value, 1, 0))
    after = jnp.where(position == depth - 1, 0.0, pltpu.roll(value, depth - 1, 0))
    scratch[line, :, 0:width] = before.astype(jnp.bfloat16)
    scratch[line, :, width : 2 * width] = value.astype(jnp.bfloat16)
    scratch[line, :, 2 * width : 3 * width] = after.astype(jnp.bfloat16)


def pack_weights(weight, packed, toward):
    ch = weight.shape[1]
    away = 2 - toward
    zero = jnp.zeros((ch, ch), jnp.bfloat16)
    for tap in range(9):
        mid_w = weight[9 + tap]
        plus_w = weight[9 * toward + tap]
        minus_w = weight[9 * away + tap]
        base = tap * 3 * ch
        packed[base : base + ch, 0:ch] = mid_w
        packed[base : base + ch, ch : 2 * ch] = minus_w
        packed[base + ch : base + 2 * ch, 0:ch] = plus_w
        packed[base + ch : base + 2 * ch, ch : 2 * ch] = mid_w
        packed[base + 2 * ch : base + 3 * ch, 0:ch] = zero
        packed[base + 2 * ch : base + 3 * ch, ch : 2 * ch] = plus_w


def lines_dot(scratch, packed, line, count):
    rows = []
    for j in range(count):
        rows.append(jnp.concatenate([scratch[line + j + dy] for dy in range(3)], axis=1))
    lhs = rows[0] if count == 1 else jnp.concatenate(rows, axis=0)
    return jnp.dot(lhs, packed[...], preferred_element_type=jnp.float32)


def lift_line(lhs, weight):
    return lax.dot_general(
        lhs, weight, (((0,), (0,)), ((), ())), preferred_element_type=jnp.float32
    )


def first_kernel(scalars, lines, lift_w, weight, bias, far, near, scratch, packed, *, block):
    ch = weight.shape[1]
    depth = far.shape[1]
    pack_weights(weight, packed, scalars[0])

    def fill(line, carry):
        store_shifted(scratch, line, elu(lift_line(lines[line], lift_w[...])))
        return carry

    lax.fori_loop(0, lines.shape[0], fill, 0)

    def step(i, carry):
        line = i * block
        act = elu(lines_dot(scratch, packed, line, block) + bias[...])
        for j in range(block):
            keep = jnp.where(scalars[1 + line + j] > 0, 1.0, 0.0)
            part = act[j * depth : (j + 1) * depth] * keep
            far[line + j] = part[:, :ch].astype(jnp.bfloat16)
            near[line + j] = part[:, ch:].astype(jnp.bfloat16)
        return carry

    lax.fori_loop(0, far.shape[0] // block, step, 0)


def second_kernel(
    scalars, far, near, halo, lines, lift_w, weight, bias, head, out, scratch, packed, *, block
):
    ch = weight.shape[1]
    pack_weights(weight, packed, scalars[0])

    def fill(line, carry):
        value = jnp.concatenate([far[line], near[line], halo[line]], axis=1)
        store_shifted(scratch, line, value.astype(jnp.float32))
        return carry

    lax.fori_loop(0, far.shape[0], fill, 0)

    def step(i, carry):
        line = i * block
        total = lines_dot(scratch, packed, line, block) + bias[...]
        lift = [lift_line(lines[line + 2 + j], lift_w[:, : 2 * ch]) for j in range(block)]
        total = total + (lift[0] if block == 1 else jnp.concatenate(lift, axis=0))
        high, low = halves(elu(total))
        contract = (((1,), (1,)), ((), ()))
        out[i] = lax.dot_general(
            head[...], high, contract, preferred_element_type=jnp.float32
        ) + lax.dot_general(head[...], low, contract, preferred_element_type=jnp.float32)
        return carry

    lax.fori_loop(0, out.shape[0], step, 0)


def block_lines(count):
    return 2 if count % 2 == 0 else 1


def params():
    return pltpu.CompilerParams(vmem_limit_bytes=VMEM_LIMIT)


def specs(kinds):
    return [
        pl.BlockSpec(memory_space=pltpu.SMEM if kind == "s" else pltpu.VMEM) for kind in kinds
    ]


def edge_lines(own):
    slab_count = lax.axis_size("slab")
    local_y = own.shape[2]
    first = lax.axis_index("coil") == 0
    near = jnp.where(first, own[:, 1:], own[:, :1])
    flat = ("slab", "coil")

    def moved(block, step, cross):
        pairs = [
            (2 * i + c, 2 * (i + step) + (1 - c if cross else c))
            for i in range(slab_count)
            for c in range(2)
            if 0 <= i + step < slab_count
        ]
        return lax.ppermute(block, flat, pairs)

    last, start = slice(local_y - 2, local_y), slice(0, 2)
    return (
        moved(own[:, :, last], 1, False),
        moved(near[:, :, last], 1, True),
        moved(own[:, :, start], -1, False),
        moved(near[:, :, start], -1, True),
    )


def score_block(
    own,
    partner,
    edges,
    lift_weight,
    lift_bias,
    conv_one,
    bias_one,
    conv_two,
    bias_two,
    head_weight,
):
    ch = lift_weight.shape[1]
    local_y, depth = own.shape[2], own.shape[3]
    coil_pos = lax.axis_index("coil")
    slab_pos = lax.axis_index("slab")
    slab_count = lax.axis_size("slab")
    first = coil_pos == 0
    low_own, low_halo, high_own, high_halo = edges
    partner_near = jnp.where(first, partner[:, :1], partner[:, 1:])
    own = jnp.concatenate([low_own, own, high_own], axis=2)
    halo = jnp.concatenate([low_halo, partner_near, high_halo], axis=2)[:, 0]
    far = jnp.where(first, own[:, 0], own[:, 1])
    near = jnp.where(first, own[:, 1], own[:, 0])
    rows = jnp.stack([far, near, halo])
    total = slab_count * local_y
    line_at = slab_pos * local_y - 2 + jnp.arange(local_y + 4, dtype=jnp.int32)
    valid = jnp.logical_and(line_at >= 0, line_at < total)
    row_hi, row_lo = split_halves(rows)
    ones = jnp.broadcast_to(
        valid.astype(jnp.bfloat16)[None, :, None], (2, local_y + 4, depth)
    )
    stacked = jnp.stack([row_hi, row_hi, row_lo], axis=2)
    stacked = stacked.reshape(18, local_y + 4, depth)
    used = jnp.concatenate([stacked, ones], axis=0)
    used = jnp.pad(used, ((0, 12), (0, 0), (0, 0)))
    lines = jnp.transpose(used, (1, 0, 2))
    w_hi = lax.reduce_precision(lift_weight, 8, 7)
    b_hi = lax.reduce_precision(lift_bias, 8, 7)
    w_rows = jnp.stack([w_hi, lift_weight - w_hi, w_hi], axis=1).reshape(6, ch)
    b_rows = jnp.stack([b_hi, lift_bias - b_hi])
    tall = jnp.concatenate([w_rows] * 3 + [b_rows, jnp.zeros((12, ch), jnp.float32)], axis=0)
    row_at = lax.broadcasted_iota(jnp.int32, (32, 3 * ch), 0)
    col_at = lax.broadcasted_iota(jnp.int32, (32, 3 * ch), 1)
    used_at = jnp.logical_or(row_at // 6 == col_at // ch, row_at >= 18)
    lift_w = jnp.where(used_at, jnp.tile(tall, (1, 3)), 0.0).astype(jnp.bfloat16)
    toward = jnp.where(first, 2, 0).astype(jnp.int32)
    scalars = jnp.concatenate([toward[None], valid[1 : local_y + 3].astype(jnp.int32)])
    block = block_lines(local_y + 2)
    scratches = lambda lines_held: [
        pltpu.VMEM((lines_held, depth, 9 * ch), jnp.bfloat16),
        pltpu.VMEM((27 * ch, 2 * ch), jnp.bfloat16),
    ]
    shape = jax.ShapeDtypeStruct((local_y + 2, depth, ch), jnp.bfloat16)
    far_two, near_two = pl.pallas_call(
        functools.partial(first_kernel, block=block),
        out_shape=(shape, shape),
        in_specs=specs("svvvv"),
        out_specs=tuple(specs("vv")),
        scratch_shapes=scratches(local_y + 4),
        compiler_params=params(),
        name="first_conv",
    )(scalars, lines, lift_w, conv_one, jnp.tile(bias_one, 2)[None])
    halo_two = swap_coil(near_two)
    h_hi, h_lo = split_halves(head_weight.T)
    zero = jnp.zeros_like(h_hi)
    wide = lambda part: jnp.concatenate(
        [jnp.concatenate([part, zero], axis=1), jnp.concatenate([zero, part], axis=1)], axis=0
    )
    head = jnp.concatenate([wide(h_hi), wide(h_lo)], axis=0)
    head = jnp.pad(head, ((0, 8), (0, 0)))
    block = block_lines(local_y)
    scored = pl.pallas_call(
        functools.partial(second_kernel, block=block),
        out_shape=jax.ShapeDtypeStruct((local_y // block, 16, block * depth), jnp.float32),
        in_specs=specs("svvvvvvvv"),
        out_specs=specs("v")[0],
        scratch_shapes=scratches(local_y + 2),
        compiler_params=params(),
        name="second_conv",
    )(
        scalars,
        far_two,
        near_two,
        halo_two,
        lines,
        lift_w,
        conv_two,
        jnp.tile(bias_two, 2)[None],
        head,
    )
    scored = scored[:, 0:4] + scored[:, 4:8]
    scored = scored.reshape(local_y // block, 2, 2, block, depth)
    scored = jnp.transpose(scored, (2, 1, 0, 3, 4)).reshape(2, 2, local_y, depth)
    return jnp.where(first, scored, scored[:, ::-1])


def tables(length):
    index = np.arange(length)
    angle = (index[:, None] * index[None, :] % length) * (2.0 * math.pi / length)

    def parts(values):
        high = values.astype(jnp.bfloat16)
        low = (values - high.astype(np.float64)).astype(jnp.bfloat16)
        return jnp.asarray(np.stack([high, low]))

    return parts(np.cos(angle)), parts(np.sin(angle))


def pair_lanes(first, second):
    depth = first.shape[-1]
    whole = depth // LANES * LANES
    tiles = [p[..., i : i + LANES] for p in (first, second) for i in range(0, whole, LANES)]
    if whole < depth:
        tiles.append(jnp.concatenate([first[..., whole:], second[..., whole:]], axis=-1))
    return jnp.stack(tiles, axis=-3)


def unpair_lanes(tiles, depth):
    count = depth // LANES
    rest = depth - count * LANES
    out = []
    for which in range(2):
        parts = tiles[which * count : (which + 1) * count]
        if rest:
            tail = tiles[2 * count]
            parts = parts + [tail[..., rest * which : rest * which + rest]]
        out.append(parts[0] if len(parts) == 1 else jnp.concatenate(parts, axis=-1))
    return out


def adjoint_kernel(planes, mask, cos_z, sin_z, cos_y, sin_y, out, total_re, total_im, *, coils):
    slabs, _, tiles, local_y, _ = planes.shape
    depth = mask.shape[1]
    whole_y = slabs * local_y

    def pair(k):
        held = [
            planes[:, k, t].reshape(whole_y, LANES).astype(jnp.float32) for t in range(tiles)
        ]
        return unpair_lanes(held, depth)

    def mm(a, b):
        return jnp.dot(a, b, preferred_element_type=jnp.float32)

    def right(a, table):
        return mm(a, table[0]) + mm(a, table[1])

    def left(table, b):
        return mm(table[0], b) + mm(table[1], b)

    total_re[...] = jnp.zeros_like(total_re)
    total_im[...] = jnp.zeros_like(total_im)

    def step(k, carry):
        map_re, map_im = pair(k)
        (u_re, u_im), (low_re, low_im) = pair(coils), pair(coils + 1)
        u_re, u_im = u_re + low_re, u_im + low_im
        c_re = (map_re * u_re - map_im * u_im).astype(jnp.bfloat16)
        c_im = (map_re * u_im + map_im * u_re).astype(jnp.bfloat16)
        f_re = (right(c_re, cos_z) + right(c_im, sin_z)).astype(jnp.bfloat16)
        f_im = (right(c_im, cos_z) - right(c_re, sin_z)).astype(jnp.bfloat16)
        m = mask[...].astype(jnp.float32)
        s_re = ((left(cos_y, f_re) + left(sin_y, f_im)) * m).astype(jnp.bfloat16)
        s_im = ((left(cos_y, f_im) - left(sin_y, f_re)) * m).astype(jnp.bfloat16)
        b_re = (left(cos_y, s_re) - left(sin_y, s_im)).astype(jnp.bfloat16)
        b_im = (left(cos_y, s_im) + left(sin_y, s_re)).astype(jnp.bfloat16)
        r_re = right(b_re, cos_z) - right(b_im, sin_z)
        r_im = right(b_im, cos_z) + right(b_re, sin_z)
        total_re[...] += map_re * r_re + map_im * r_im
        total_im[...] += map_re * r_im - map_im * r_re
        return carry

    lax.fori_loop(0, coils, step, 0)
    shape = (slabs, local_y, LANES)
    count = depth // LANES
    for t in range(count):
        lanes = slice(t * LANES, (t + 1) * LANES)
        out[:, t] = total_re[:, lanes].reshape(shape)
        out[:, count + t] = total_im[:, lanes].reshape(shape)
    if tiles > 2 * count:
        tail = jnp.concatenate([total_re[:, count * LANES :], total_im[:, count * LANES :]], axis=1)
        out[:, 2 * count] = tail.reshape(shape)


def own_share(partial):
    rows = partial.shape[1] // 2
    first = lax.axis_index("coil") == 0
    lower, upper = partial[:, :rows], partial[:, rows:]
    received = swap_coil(jnp.where(first, upper, lower))
    return jnp.where(first, lower, upper) + received


def map_planes(whole, coil_maps):
    slabs = lax.axis_size("slab")
    _, local_coils, readout, local_y, depth = coil_maps.shape
    coil_blocks = slabs // readout
    coils = local_coils // coil_blocks
    maps = pair_lanes(coil_maps[0], coil_maps[1])
    maps = maps.reshape(coil_blocks, coils, readout, *maps.shape[2:])
    maps = jnp.swapaxes(maps, 1, 2).reshape(slabs, coils, *maps.shape[3:])
    u = jnp.stack([pair_lanes(part[0], part[1]) for part in split_halves(whole)], axis=1)
    return jnp.concatenate([maps, jnp.tile(u, (coil_blocks, 1, 1, 1, 1))], axis=1)


def exchanged(value):
    return lax.all_to_all(value, "slab", split_axis=0, concat_axis=0, tiled=True)


def adjoint_by_slice(planes, readout, sampled_lines):
    slabs, count, tiles, local_y, _ = planes.shape
    whole_y, depth = sampled_lines.shape
    combined = pl.pallas_call(
        functools.partial(adjoint_kernel, coils=count - 2),
        out_shape=jax.ShapeDtypeStruct((slabs, tiles, local_y, LANES), jnp.float32),
        in_specs=specs("vvvvvv"),
        out_specs=specs("v")[0],
        scratch_shapes=[pltpu.VMEM((whole_y, depth), jnp.float32)] * 2,
        compiler_params=params(),
        name="adjoint",
    )(planes, sampled_lines, *tables(depth), *tables(whole_y))
    returned = exchanged(combined)
    returned = returned.reshape(slabs // readout, readout, tiles, local_y, LANES)
    partial = jnp.sum(returned, axis=0)
    partial = jnp.stack(unpair_lanes([partial[:, t] for t in range(tiles)], depth))
    return own_share(partial * (1.0 / (whole_y * depth)))


def float_tables(length):
    index = np.arange(length)
    angle = (index[:, None] * index[None, :] % length) * (2.0 * math.pi / length)
    scale = 1.0 / math.sqrt(length)
    return (
        jnp.asarray((np.cos(angle) * scale).astype(np.float32)),
        jnp.asarray((np.sin(angle) * scale).astype(np.float32)),
    )


def adjoint_by_columns(whole, coil_maps, sampled_lines):
    slabs = lax.axis_size("slab")
    slab_pos = lax.axis_index("slab")
    _, local_coils, readout, local_y, depth = coil_maps.shape
    slices = local_coils * readout
    z_blocks = max(1, slabs // math.gcd(slabs, slices))
    width = depth // z_blocks
    maps = coil_maps.astype(jnp.float32)
    map_re, map_im = maps[0], maps[1]
    coil_re = map_re * whole[0][None] - map_im * whole[1][None]
    coil_im = map_re * whole[1][None] + map_im * whole[0][None]
    cos_z, sin_z = (t.reshape(depth, z_blocks, width) for t in float_tables(depth))
    cos_y, sin_y = float_tables(slabs * local_y)
    ein = functools.partial(jnp.einsum, precision=lax.Precision.HIGHEST)
    out = "cxyz,zbk->bcxyk"
    f_re = ein(out, coil_re, cos_z) + ein(out, coil_im, sin_z)
    f_im = ein(out, coil_im, cos_z) - ein(out, coil_re, sin_z)
    each = z_blocks * slices // slabs

    def there(value):
        value = value.reshape(slabs, each, local_y, width).astype(jnp.bfloat16)
        value = lax.all_to_all(value, "slab", split_axis=0, concat_axis=2, tiled=True)
        return value.astype(jnp.float32)

    def back(value):
        value = value.astype(jnp.bfloat16)
        value = lax.all_to_all(value, "slab", split_axis=2, concat_axis=0, tiled=True)
        value = value.astype(jnp.float32)
        return value.reshape(z_blocks, local_coils, readout, local_y, width)

    p_re, p_im = there(f_re), there(f_im)
    block = slab_pos * each // slices
    mask = lax.dynamic_slice_in_dim(sampled_lines.astype(jnp.float32), block * width, width, 1)
    go = "qy,aiyk->aiqk"
    s_re = (ein(go, cos_y, p_re) + ein(go, sin_y, p_im)) * mask
    s_im = (ein(go, cos_y, p_im) - ein(go, sin_y, p_re)) * mask
    home = "qy,aiqk->aiyk"
    b_re = back(ein(home, cos_y, s_re) - ein(home, sin_y, s_im))
    b_im = back(ein(home, cos_y, s_im) + ein(home, sin_y, s_re))
    fin = "bcxyk,zbk->cxyz"
    r_re = ein(fin, b_re, cos_z) - ein(fin, b_im, sin_z)
    r_im = ein(fin, b_im, cos_z) + ein(fin, b_re, sin_z)
    partial = jnp.stack(
        [
            jnp.sum(map_re * r_re + map_im * r_im, axis=0),
            jnp.sum(map_re * r_im - map_im * r_re, axis=0),
        ]
    )
    return own_share(partial)


def local(
    image,
    noise,
    coil_maps,
    adjoint_data,
    sampled_lines,
    lift_weight,
    lift_bias,
    conv_one,
    bias_one,
    conv_two,
    bias_two,
    head_weight,
    head_bias,
):
    slabs = lax.axis_size("slab")
    local_coils, readout = coil_maps.shape[1:3]
    partner = swap_coil(image)
    first = lax.axis_index("coil") == 0
    whole = jnp.where(
        first,
        jnp.concatenate([image, partner], axis=1),
        jnp.concatenate([partner, image], axis=1),
    )
    depth = image.shape[3]
    by_slice = slabs % readout == 0 and local_coils % (slabs // readout) == 0
    by_slice = by_slice and depth % LANES in (0, LANES // 2)
    edges = edge_lines(image)
    if by_slice:
        planes = map_planes(whole, coil_maps)
        planes, edges = lax.optimization_barrier((planes, edges))
        planes = exchanged(planes)
    score = score_block(
        image,
        partner,
        edges,
        lift_weight,
        lift_bias,
        conv_one,
        bias_one,
        conv_two,
        bias_two,
        head_weight,
    )
    score = (score + head_bias[:, None, None, None]) / noise_level
    if by_slice:
        planes, score = lax.optimization_barrier((planes, score))
        adjoint = adjoint_by_slice(planes, readout, sampled_lines)
    else:
        adjoint = adjoint_by_columns(whole, coil_maps, sampled_lines)
    dc_gradient = adjoint - adjoint_data
    next_image = (
        image + step_size * (score - data_weight * dc_gradient) + math.sqrt(2.0 * step_size) * noise
    )
    return (next_image, dc_gradient)


def solution(mesh):
    image_spec = P(None, ("group", "coil"), "slab", None)
    return jax.shard_map(
        local,
        mesh=mesh,
        in_specs=(
            image_spec,
            image_spec,
            P(None, "coil", "group", "slab", None),
            image_spec,
            P("group", None),
        )
        + (P(),) * 8,
        out_specs=(image_spec, image_spec),
        check_vma=False,
    )
```

time: 458 us -> 135 us (0.29)
  matrix products: 203 us -> 0 us
  local copies, waits for them, and re-layouts: 126 us -> 9.47 us
  Pallas kernels: 0 us -> 73.9 us
  starting transfers between devices: 53.4 us -> 20.6 us
  other arithmetic: 36 us -> 7.8 us
  blocking collectives: 2.3 us -> 16.5 us
  between operations: 15.1 us -> 1.19 us
  waiting for transfers between devices: 16 us -> 3.03 us
    dot_general x36 -> x0, matrix products: 203 us -> none  [the longest x18 124 us: convolve(): jnp.einsum('xyzc,cd->xyzd', columns, stacked[3 * shift_x + shift_y], pref...]
    slice x11, local copies, waits for them, and re-layouts: 103 us -> 1.29 us  [the longest x1 0.78 us: edge_lines(): own[:, :, start]]
    pallas_call x0 -> x3, Pallas kernels: none -> 73.9 us  [the longest x1 30 us: score_block(): pl.pallas_call(functools.partial(first_kernel, block=block), out_shape=(s...]
    concatenate x6 -> x5, other arithmetic: 29 us -> 2.42 us  [the longest x1 1.47 us: map_planes(): jnp.concatenate([maps, jnp.tile(u, (coil_blocks, 1, 1, 1, 1))], axis=1)]
    all_to_all x4 -> x1, starting transfers between devices: 27.7 us -> 7.25 us  [exchanged(): lax.all_to_all(value, 'slab', split_axis=0, concat_axis=0, tiled=True)]
    all_to_all x0 -> x1, blocking collectives: none -> 16.5 us  [exchanged(): lax.all_to_all(value, 'slab', split_axis=0, concat_axis=0, tiled=True)]
    ppermute x8 -> x7, starting transfers between devices: 25.7 us -> 13.3 us  [the longest x4 10.5 us: moved(): return lax.ppermute(block, flat, pairs)]
    ppermute x8 -> x7, waiting for transfers between devices: 13.6 us -> 3.03 us  [the longest x3 3.02 us: swap_coil(): return lax.ppermute(value, 'coil', [(0, 1), (1, 0)])]
  transfers between devices with their start and end apart: 13 -> 8, of which waited for: 3 -> 2; matrix products, arithmetic and copies ran while one was open for 76% -> 10% of each run, Pallas kernels for 0% -> 43%
where the time goes in v1:
time: 135 us; the launch traced here: 133 us
  Pallas kernels  73.9 us (55%)
  starting transfers between devices  20.6 us (15%)
  blocking collectives  16.5 us (12%)
  local copies, waits for them, and re-layouts  9.47 us (7%)
  other arithmetic  7.8 us (6%)
  waiting for transfers between devices  3.03 us (2%)
    pallas_call x1, Pallas kernels, score_block(): pl.pallas_call(functools.partial(first_kernel, block=block), out_shape=(s...  30 us
    pallas_call x1, Pallas kernels, score_block(): pl.pallas_call(functools.partial(second_kernel, block=block), out_shape=j...  27.1 us
    pallas_call x1, Pallas kernels, adjoint_by_slice(): pl.pallas_call(functools.partial(adjoint_kernel, coils=count - 2), out_sh...  16.9 us
    all_to_all x1, blocking collectives, exchanged(): lax.all_to_all(value, 'slab', split_axis=0, concat_axis=0, tiled=True)  16.5 us
    ppermute x4, starting transfers between devices, moved(): return lax.ppermute(block, flat, pairs)  10.5 us
    all_to_all x1, starting transfers between devices, exchanged(): lax.all_to_all(value, 'slab', split_axis=0, concat_axis=0, tiled=True)  7.25 us
    unnamed x24, local copies, waits for them, and re-layouts  3.45 us
    ppermute x3, waiting for transfers between devices, swap_coil(): return lax.ppermute(value, 'coil', [(0, 1), (1, 0)])  3.02 us
  transfers between devices with their start and end apart: 8, of which 2 were waited for; matrix products, arithmetic and copies ran while one was open for 10% of the time, Pallas kernels for 43%

profile of v1, /device:TPU:3, one launch (start us, length us, event | category | flops | bytes accessed | tf_op | source)
XLA Modules:
  0.0 132.5 jit_solution(238046059699282742)
XLA Ops:
  0.6 0.9 copy.53
  1.5 0.7 collective-permute-start
  2.3 0.8 fusion.27
  3.1 3.2 %collective-permute-start.1 = (f32[2,2,2,192]{3,2,0,1:T(2,128)S(1)}, f32[2,2,2,192]{3,2,0,1:T(2,128)S(1)}, u32[]{:S(2)}, u32[]{:S(2)}) collective-permute-start(f32[2,2,2,192]{3,2,0,1:T(2,128)S(1)} %get-tuple-element.34), channel_id=1, source_target_pairs={{0,2},{1,3},{2,4},{3,5},{4,6},{5,7},{6,8},{7,9},{8,10},{9,11},{10,... | collective-permute-start | bytes 18440 | tf_op jit(solution)/shard_map/ppermute | solution.py:159
  6.2 0.9 slice_select_fusion.2
  7.2 3.3 %collective-permute-start.2 = (f32[2,1,2,192]{3,2,0,1:T(2,128)S(1)}, f32[2,1,2,192]{3,2,0,1:T(2,128)S(1)}, u32[]{:S(2)}, u32[]{:S(2)}) collective-permute-start(f32[2,1,2,192]{3,2,0,1:T(2,128)S(1)} %get-tuple-element.42), channel_id=1, source_target_pairs={{0,3},{1,2},{2,5},{3,4},{4,7},{5,6},{6,9},{7,8},{8,11},{9,10},{10,... | collective-permute-start | bytes 9224 | tf_op jit(solution)/shard_map/ppermute | solution.py:159
  10.5 2.2 %collective-permute-start.3 = (f32[2,2,2,192]{3,2,0,1:T(2,128)S(1)}, f32[2,2,2,192]{3,2,0,1:T(2,128)S(1)}, u32[]{:S(2)}, u32[]{:S(2)}) collective-permute-start(f32[2,2,2,192]{3,2,0,1:T(2,128)S(1)} %get-tuple-element.33), channel_id=1, source_target_pairs={{2,0},{3,1},{4,2},{5,3},{6,4},{7,5},{8,6},{9,7},{10,8},{11,9},{12,... | collective-permute-start | bytes 18440 | tf_op jit(solution)/shard_map/ppermute | solution.py:159
  12.6 1.9 %collective-permute-start.4 = (f32[2,1,2,192]{3,2,0,1:T(2,128)S(1)}, f32[2,1,2,192]{3,2,0,1:T(2,128)S(1)}, u32[]{:S(2)}, u32[]{:S(2)}) collective-permute-start(f32[2,1,2,192]{3,2,0,1:T(2,128)S(1)} %get-tuple-element.41), channel_id=1, source_target_pairs={{2,1},{3,0},{4,3},{5,2},{6,5},{7,4},{8,7},{9,6},{10,9},{11,8},{12,... | collective-permute-start | bytes 9224 | tf_op jit(solution)/shard_map/ppermute | solution.py:159
  14.6 1.7 %slice_bitcast_fusion.1 = (bf16[16,4,32,192]{3,2,1,0:T(8,128)(2,1)S(1)}, bf16[16,4,32,192]{3,2,1,0:T(8,128)(2,1)S(1)}) fusion(bf16[2,16,4,32,192]{4,3,2,1,0:T(8,128)(2,1)} %param.19), kind=kLoop, calls=%fused_computation.6 | loop fusion | bytes 3145728 | tf_op jit(solution)/shard_map/squeeze | solution.py:368
  17.3 0.3 copy.71
  17.6 0.3 copy-done.5
  18.0 0.3 concatenate.82
  18.4 0.7 fusion.8.lift_w
  19.7 1.5 %pad_maximum_fusion = bf16[8,10,3,32,128]{4,3,2,1,0:T(8,128)(2,1)} fusion(bf16[8,2,3,32,128]{4,3,2,1,0:T(8,128)(2,1)S(1)} %bitcast.88, bf16[8,8,3,32,128]{4,3,2,1,0:T(8,128)(2,1)S(1)} %bitcast.83), kind=kLoop, calls=%fused_computation | loop fusion | flops 983040 | bytes 3932160 | tf_op jit(solution)/shard_map/concatenate | solution.py:372
  21.2 7.3 %all-to-all-start = ((bf16[8,10,3,32,128]{4,3,2,1,0:T(8,128)(2,1)}), bf16[8,10,3,32,128]{4,3,2,1,0:T(8,128)(2,1)S(1)}, u32[]{:S(2)}, u32[]{:S(2)}) async-start(bf16[8,10,3,32,128]{4,3,2,1,0:T(8,128)(2,1)} %pad_maximum_fusion), calls=%async_computation | async-start | bytes 3932160 | tf_op jit(solution)/shard_map/all_to_all | solution.py:376
  28.5 0.6 pad_add_fusion.scalars
  29.6 1.0 fusion.3.lines
  30.6 0.6 tile.16
  31.2 30.0 %first_conv.1 = (bf16[34,192,128]{2,1,0:T(8,128)(2,1)}, bf16[34,192,128]{2,1,0:T(8,128)(2,1)}) custom-call(s32[35]{0:T(128)} %pad_add_fusion.scalars, bf16[36,32,192]{2,1,0:T(8,128)(2,1)} %fusion.3.lines, bf16[32,384]{1,0:T(8,128)(2,1)} %fusion.8.lift_w, bf16[27,128,128]{2,1,0:T(8,128)(2,1)} %weight.2, f32[1,256]{1,0:T(1,128)} %bitcast.93), custom_call_target="tpu_custom_call" | custom-call | tf_op jit(solution)/shard_map/first_conv/pallas_call | solution.py:224
  61.1 0.6 collective-permute-start.5
  61.7 0.9 copy.68.mask
  62.6 0.6 pad.13.head
  63.2 2.0 %collective-permute-done.5.halo = bf16[34,192,128]{2,1,0:T(8,128)(2,1)} collective-permute-done((bf16[34,192,128]{2,1,0:T(8,128)(2,1)}, bf16[34,192,128]{2,1,0:T(8,128)(2,1)}, u32[]{:S(2)}, u32[]{:S(2)}) %collective-permute-start.5) | collective-permute-done | bytes 1671200 | tf_op jit(solution)/shard_map/ppermute | solution.py:35
  65.2 0.6 tile.17
  65.8 27.1 %second_conv.1 = f32[16,16,384]{2,1,0:T(8,128)} custom-call(s32[35]{0:T(128)} %pad_add_fusion.scalars, bf16[34,192,128]{2,1,0:T(8,128)(2,1)} %get-tuple-element.16.far, bf16[34,192,128]{2,1,0:T(8,128)(2,1)} %get-tuple-element.17.near, bf16[34,192,128]{2,1,0:T(8,128)(2,1)} %collective-permute-done.5.halo, bf16[36,32,192]{2,1,0:T(8,128)(2,1)} %fusion.3.lines, ...), custom_call_target="tpu_custom_call" | custom-call | tf_op jit(solution)/shard_map/second_conv/pallas_call | solution.py:242
  92.9 1.0 slice_add_fusion
  94.3 1.3 copy-done
  95.6 16.9 %adjoint.1 = f32[8,3,32,128]{3,2,1,0:T(8,128)} custom-call(bf16[8,10,3,32,128]{4,3,2,1,0:T(8,128)(2,1)} %copy-done, s32[256,192]{1,0:T(8,128)} %copy.68.mask, bf16[2,192,192]{2,1,0:T(8,128)(2,1)} %constant.70.clone.cos_z, bf16[2,192,192]{2,1,0:T(8,128)(2,1)} %constant.71.clone.sin_z, bf16[2,256,256]{2,1,0:T(8,128)(2,1)} %constant.72.clone.cos_y, ...), custom_call_target="tpu_custom_call" | custom-call | tf_op jit(solution)/shard_map/adjoint/pallas_call | solution.py:382
  112.5 16.5 %all_to_all.10 = f32[8,3,32,128]{3,2,1,0:T(8,128)S(1)} all-to-all(f32[8,3,32,128]{3,2,1,0:T(8,128)} %adjoint.1), channel_id=1, replica_groups=mesh['group'=2,'slab'=8,'coil'=2] {'slab'}, dimensions={0} | all-to-all | bytes 786432 | tf_op jit(solution)/shard_map/all_to_all | solution.py:376
  129.3 1.5 %collective-permute-start.6 = (f32[2,2,32,192]{3,2,1,0:T(8,128)S(1)}, f32[2,2,32,192]{3,2,1,0:T(8,128)S(1)}, u32[]{:S(2)}, u32[]{:S(2)}) collective-permute-start(f32[2,2,32,192]{3,2,1,0:T(8,128)S(1)} %slice_select_fusion), channel_id=1, source_target_pairs={{0,1},{1,0},{2,3},{3,2},{4,5},{5,4},{6,7},{7,6},{8,9},{9,8},{10,11... | collective-permute-start | bytes 294920 | tf_op jit(solution)/shard_map/ppermute | solution.py:35
  130.8 1.0 collective-permute-done.6
  131.8 0.8 multiply_add_fusion
  (85 shorter events, 2.5 us)
Async XLA Ops:
  1.5 17.5 %collective-permute-start = (f32[2,2,32,192]{3,2,0,1:T(8,128)S(1)}, f32[2,2,32,192]{3,2,0,1:T(8,128)S(1)}, u32[]{:S(2)}, u32[]{:S(2)}) collective-permute-start(f32[2,2,32,192]{3,2,0,1:T(8,128)S(1)} %copy.53), channel_id=1, source_target_pairs={{0,1},{1,0},{2,3},{3,2},{4,5},{5,4},{6,7},{7,6},{8,9},{9,8},{10,11... | collective-permute-start | bytes 294920 | tf_op jit(solution)/shard_map/ppermute | solution.py:35
  3.1 18.1 %collective-permute-start.1 = (f32[2,2,2,192]{3,2,0,1:T(2,128)S(1)}, f32[2,2,2,192]{3,2,0,1:T(2,128)S(1)}, u32[]{:S(2)}, u32[]{:S(2)}) collective-permute-start(f32[2,2,2,192]{3,2,0,1:T(2,128)S(1)} %get-tuple-element.34), channel_id=1, source_target_pairs={{0,2},{1,3},{2,4},{3,5},{4,6},{5,7},{6,8},{7,9},{8,10},{9,11},{10,... | collective-permute-start | bytes 18440 | tf_op jit(solution)/shard_map/ppermute | solution.py:159
  7.2 14.0 %collective-permute-start.2 = (f32[2,1,2,192]{3,2,0,1:T(2,128)S(1)}, f32[2,1,2,192]{3,2,0,1:T(2,128)S(1)}, u32[]{:S(2)}, u32[]{:S(2)}) collective-permute-start(f32[2,1,2,192]{3,2,0,1:T(2,128)S(1)} %get-tuple-element.42), channel_id=1, source_target_pairs={{0,3},{1,2},{2,5},{3,4},{4,7},{5,6},{6,9},{7,8},{8,11},{9,10},{10,... | collective-permute-start | bytes 9224 | tf_op jit(solution)/shard_map/ppermute | solution.py:159
  10.5 10.7 %collective-permute-start.3 = (f32[2,2,2,192]{3,2,0,1:T(2,128)S(1)}, f32[2,2,2,192]{3,2,0,1:T(2,128)S(1)}, u32[]{:S(2)}, u32[]{:S(2)}) collective-permute-start(f32[2,2,2,192]{3,2,0,1:T(2,128)S(1)} %get-tuple-element.33), channel_id=1, source_target_pairs={{2,0},{3,1},{4,2},{5,3},{6,4},{7,5},{8,6},{9,7},{10,8},{11,9},{12,... | collective-permute-start | bytes 18440 | tf_op jit(solution)/shard_map/ppermute | solution.py:159
  12.6 8.5 %collective-permute-start.4 = (f32[2,1,2,192]{3,2,0,1:T(2,128)S(1)}, f32[2,1,2,192]{3,2,0,1:T(2,128)S(1)}, u32[]{:S(2)}, u32[]{:S(2)}) collective-permute-start(f32[2,1,2,192]{3,2,0,1:T(2,128)S(1)} %get-tuple-element.41), channel_id=1, source_target_pairs={{2,1},{3,0},{4,3},{5,2},{6,5},{7,4},{8,7},{9,6},{10,9},{11,8},{12,... | collective-permute-start | bytes 9224 | tf_op jit(solution)/shard_map/ppermute | solution.py:159
  17.2 0.7 copy-start.5
  17.3 0.7 copy-start.8
  17.3 1.8 %copy-start.1 = (f32[2,2,32,192]{3,2,1,0:T(8,128)S(1)}, f32[2,2,32,192]{3,2,1,0:T(8,128)}, u32[]{:S(2)}) copy-start(f32[2,2,32,192]{3,2,1,0:T(8,128)} %param.17) | copy-start | bytes 294916
  21.2 73.1 %all-to-all-start = ((bf16[8,10,3,32,128]{4,3,2,1,0:T(8,128)(2,1)}), bf16[8,10,3,32,128]{4,3,2,1,0:T(8,128)(2,1)S(1)}, u32[]{:S(2)}, u32[]{:S(2)}) async-start(bf16[8,10,3,32,128]{4,3,2,1,0:T(8,128)(2,1)} %pad_maximum_fusion), calls=%async_computation | async-start | bytes 3932160 | tf_op jit(solution)/shard_map/all_to_all | solution.py:376
  29.2 1.4 %copy-start.9 = (f32[128]{0:T(128)S(1)}, f32[128]{0:T(128)}, u32[]{:S(2)}) copy-start(f32[128]{0:T(128)} %param.25) | copy-start | bytes 1540
  29.4 32.4 %copy-start.2 = (s32[256,192]{0,1:T(8,128)S(1)}, s32[256,192]{0,1:T(8,128)}, u32[]{:S(2)}) copy-start(s32[256,192]{0,1:T(8,128)} %param.21) | copy-start | bytes 589828
  29.5 33.1 %copy-start.6 = (f32[128,2]{0,1:T(2,128)S(1)}, f32[128,2]{0,1:T(2,128)}, u32[]{:S(2)}) copy-start(f32[128,2]{0,1:T(2,128)} %param.28) | copy-start | bytes 3076
  29.5 35.8 %copy-start.10 = (f32[128]{0:T(128)S(1)}, f32[128]{0:T(128)}, u32[]{:S(2)}) copy-start(f32[128]{0:T(128)} %param.27) | copy-start | bytes 1540
  61.1 4.1 %collective-permute-start.5 = (bf16[34,192,128]{2,1,0:T(8,128)(2,1)}, bf16[34,192,128]{2,1,0:T(8,128)(2,1)}, u32[]{:S(2)}, u32[]{:S(2)}) collective-permute-start(bf16[34,192,128]{2,1,0:T(8,128)(2,1)} %get-tuple-element.17.near), channel_id=1, source_target_pairs={{0,1},{1,0},{2,3},{3,2},{4,5},{5,4},{6,7},{7,6},{8,9},{9,8},{10,11... | collective-permute-start | bytes 5013512 | tf_op jit(solution)/shard_map/ppermute | solution.py:35
  65.8 28.4 %copy-start.7 = (f32[2]{0:T(128)S(1)}, f32[2]{0:T(128)}, u32[]{:S(2)}) copy-start(f32[2]{0:T(128)} %param.29) | copy-start | bytes 28
  94.3 1.3 copy-start
  112.5 19.2 %copy-start.3 = (f32[2,2,32,192]{3,2,1,0:T(8,128)S(1)}, f32[2,2,32,192]{3,2,1,0:T(8,128)}, u32[]{:S(2)}) copy-start(f32[2,2,32,192]{3,2,1,0:T(8,128)} %param.18) | copy-start | bytes 294916
  112.5 19.2 %copy-start.4 = (f32[2,2,32,192]{3,2,1,0:T(8,128)S(1)}, f32[2,2,32,192]{3,2,1,0:T(8,128)}, u32[]{:S(2)}) copy-start(f32[2,2,32,192]{3,2,1,0:T(8,128)} %param.20) | copy-start | bytes 294916
  129.3 2.5 %collective-permute-start.6 = (f32[2,2,32,192]{3,2,1,0:T(8,128)S(1)}, f32[2,2,32,192]{3,2,1,0:T(8,128)S(1)}, u32[]{:S(2)}, u32[]{:S(2)}) collective-permute-start(f32[2,2,32,192]{3,2,1,0:T(8,128)S(1)} %slice_select_fusion), channel_id=1, source_target_pairs={{0,1},{1,0},{2,3},{3,2},{4,5},{5,4},{6,7},{7,6},{8,9},{9,8},{10,11... | collective-permute-start | bytes 294920 | tf_op jit(solution)/shard_map/ppermute | solution.py:35
